TPU v7x, 32 devices: a whole 2x2x4 slice. The times are simulated.
32 devices in a mesh: pts: 16 (over z, x, core), proto: 2 (over y).
Axes of the slice: x: 2, y: 2, z: 4, core: 2. Of those that a mesh axis runs over, the one named last changes fastest.
Arguments:
- points: bfloat16 [128, 128, 1024], P('pts', None, 'proto'), as said below
- prototypes: bfloat16 [32, 512, 1024], P(('pts', 'proto')), as said below
- coarse_duals: float32 [32, 512], P(('pts', 'proto')), may hold values from -8 to 8
- active: int32 [128, 8], P('pts'), may hold values from 0 to 31, as said below
Outputs:
- point_duals: float32 [128, 128], P('pts')
- new_duals: float32 [32, 512], P(('pts', 'proto'))
Inputs may be any that keep to these rules, and one draw needn't show every extreme that they name: `active`: each row names 8 different blocks. Block b belongs to owner group b // 2. The 8 rows of one index of pts name any one owner group at most 8 times, and exactly that often for 8 groups. Over all rows every owner group is named 64 times in all, every block at least once and at most 32 times, and in every owner group some block exactly 32 times. `points`: Real-valued embeddings. `prototypes`: Real-valued embeddings.
All inputs are finite; a program needn't handle non-finite values.
Results may differ from a plain program's by a relative error of at most 0.0003.
Values may be sent and summed in bfloat16 or wider, within the bound.
A program may use at most 128 MiB of HBM per device.

v0:
```python
import jax
import jax.numpy as jnp
from jax import lax
from jax.sharding import PartitionSpec as P

LOWEST = -1e30


def body(points, prototypes, coarse_duals, active):
    groups = lax.axis_size("pts")
    owners = lax.axis_size("proto")
    blocks, row_count, slice_width = points.shape
    active_width = active.shape[1]
    pair_total = blocks * active_width
    capacity = max(2, 2 * pair_total // groups)
    bucket_cap = 3 * pair_total // (owners + 4)
    slot_count = groups * capacity
    pair_ids = jnp.arange(pair_total, dtype=jnp.int32)
    slot_ids = jnp.arange(slot_count, dtype=jnp.int32)
    targets = active.reshape(pair_total)
    dest_group = targets // owners
    dest_local = targets % owners
    before = (dest_group[:, None] == dest_group[None, :]) & (pair_ids[None, :] < pair_ids[:, None])
    slot_of_pair = dest_group * capacity + jnp.sum(before.astype(jnp.int32), axis=1)
    slot_hits = slot_of_pair[None, :] == slot_ids[:, None]
    filled = jnp.any(slot_hits, axis=1)
    pair_of_slot = jnp.sum(jnp.where(slot_hits, pair_ids[None, :], 0), axis=1)
    block_of_slot = pair_of_slot // active_width
    send_tag = jnp.where(filled, dest_local[pair_of_slot], owners)
    outgoing = jnp.where(filled[:, None, None], points[block_of_slot], jnp.zeros((), points.dtype))
    arrived, arrived_tag = (
        lax.all_to_all(
            outgoing.reshape(groups, capacity, row_count, slice_width),
            "pts",
            split_axis=0,
            concat_axis=0,
            tiled=True,
        ),
        lax.all_to_all(
            send_tag.reshape(groups, capacity), "pts", split_axis=0, concat_axis=0, tiled=True
        ),
    )
    arrived = arrived.reshape(slot_count, row_count, slice_width)
    arrived_tag = arrived_tag.reshape(slot_count)
    occupied = arrived_tag < owners
    earlier_slots = (arrived_tag[None, :] == arrived_tag[:, None]) & (
        slot_ids[None, :] < slot_ids[:, None]
    )
    position = jnp.sum(earlier_slots.astype(jnp.int32), axis=1)
    bucket_code = jnp.where(occupied, arrived_tag * bucket_cap + position, owners * bucket_cap)
    bucket_ids = jnp.arange(owners * bucket_cap, dtype=jnp.int32)
    bucket_match = bucket_code[None, :] == bucket_ids[:, None]
    taken = jnp.any(bucket_match, axis=1)
    slot_of_bucket = jnp.sum(jnp.where(bucket_match, slot_ids[None, :], 0), axis=1)
    sectioned = jnp.where(
        taken[:, None, None], arrived[slot_of_bucket], jnp.zeros((), arrived.dtype)
    )
    resident = lax.all_to_all(
        sectioned.reshape(owners, bucket_cap, row_count, slice_width),
        "proto",
        split_axis=0,
        concat_axis=3,
        tiled=True,
    )
    resident = resident.reshape(bucket_cap, row_count, slice_width * owners)
    my_index = lax.axis_index("proto")
    my_taken = lax.dynamic_slice_in_dim(taken.reshape(owners, bucket_cap), my_index, 1, 0)[0]
    my_slot = lax.dynamic_slice_in_dim(slot_of_bucket.reshape(owners, bucket_cap), my_index, 1, 0)[
        0
    ]
    owned_block = prototypes[0]
    scores = jnp.einsum("hrd,cd->hrc", resident, owned_block, preferred_element_type=jnp.float32)
    shifted = scores + coarse_duals[0][None, None, :]
    row_peak = jnp.max(shifted, axis=2)
    row_mass = jnp.sum(jnp.exp(shifted - row_peak[:, :, None]), axis=2)
    all_peak, all_mass = (
        lax.all_gather(row_peak[None], "proto", axis=0, tiled=True),
        lax.all_gather(row_mass[None], "proto", axis=0, tiled=True),
    )
    all_peak = all_peak.reshape(owners * bucket_cap, row_count)
    all_mass = all_mass.reshape(owners * bucket_cap, row_count)
    lookup = jnp.where(occupied, bucket_code, 0)
    back_peak = jnp.where(occupied[:, None], all_peak[lookup], LOWEST)
    back_mass = jnp.where(occupied[:, None], all_mass[lookup], 0.0)
    got_peak, got_mass = (
        lax.all_to_all(
            back_peak.reshape(groups, capacity, row_count),
            "pts",
            split_axis=0,
            concat_axis=0,
            tiled=True,
        ),
        lax.all_to_all(
            back_mass.reshape(groups, capacity, row_count),
            "pts",
            split_axis=0,
            concat_axis=0,
            tiled=True,
        ),
    )
    pair_peak = got_peak.reshape(slot_count, row_count)[slot_of_pair].reshape(
        blocks, active_width, row_count
    )
    pair_mass = got_mass.reshape(slot_count, row_count)[slot_of_pair].reshape(
        blocks, active_width, row_count
    )
    peak = jnp.max(pair_peak, axis=1)
    mass = jnp.sum(pair_mass * jnp.exp(pair_peak - peak[:, None, :]), axis=1)
    point_duals = -(peak + jnp.log(mass))
    outgoing_duals = jnp.where(filled[:, None], point_duals[block_of_slot], 0.0)
    arrived_duals = lax.all_to_all(
        outgoing_duals.reshape(groups, capacity, row_count),
        "pts",
        split_axis=0,
        concat_axis=0,
        tiled=True,
    )
    my_duals = arrived_duals.reshape(slot_count, row_count)[my_slot]
    rescored = jnp.einsum(
        "hrd,cd->hrc",
        lax.optimization_barrier(resident),
        owned_block,
        preferred_element_type=jnp.float32,
    )
    column_arg = jnp.where(my_taken[:, None, None], rescored + my_duals[:, :, None], LOWEST)
    col_peak = jnp.max(column_arg, axis=(0, 1))
    col_mass = jnp.sum(jnp.exp(column_arg - col_peak[None, None, :]), axis=(0, 1))
    new_duals = -(col_peak + jnp.log(col_mass))
    return (point_duals, new_duals[None, :])


def solution(mesh):
    return jax.shard_map(
        body,
        mesh=mesh,
        in_specs=(
            P("pts", None, "proto"),
            P(("pts", "proto"), None, None),
            P(("pts", "proto"), None),
            P("pts", None),
        ),
        out_specs=(P("pts", None), P(("pts", "proto"), None)),
        check_vma=False,
    )
```

profile of v0, /device:TPU:0, one launch (start us, length us, event | category | flops | bytes accessed | tf_op | source)
XLA Modules:
  0.0 616.1 jit_solution(16729566166568876897)
XLA Ops:
  0.6 0.9 reshape.444
  1.9 1.2 gather_fusion
  3.2 0.7 select_n.191
  3.9 7.4 %all-to-all-start = ((s32[16,1,8]{2,1,0:T(1,128)}), s32[16,1,8]{2,1,0:T(1,128)S(1)}, u32[]{:S(2)}, u32[]{:S(2)}) async-start(s32[16,1,8]{2,1,0:T(1,128)} %bitcast.2), calls=%async_computation | async-start | bytes 16384 | tf_op jit(solution)/shard_map/all_to_all | solution.py:39
  11.3 8.1 %gather_fusion.1 = bf16[128,128,512]{2,1,0:T(8,128)(2,1)} fusion(bf16[8,128,512]{2,1,0:T(8,128)(2,1)S(1)} %copy-done, s32[1024]{0:T(1024)S(1)} %get-tuple-element.14), kind=kCustom, calls=%fused_computation.1 | custom fusion | bytes 33554944 | tf_op jit(solution)/shard_map/gather | solution.py:30
  19.4 14.0 %broadcast_select_fusion = bf16[16,8,128,512]{3,2,1,0:T(8,128)(2,1)} fusion(bf16[16,8,128,512]{3,2,1,0:T(8,128)(2,1)} %bitcast.84, pred[16,8]{1,0:T(8,128)(4,1)S(1)} %broadcast_in_dim.142), kind=kLoop, calls=%fused_computation.9 | loop fusion | flops 8388608 | bytes 33554560 | tf_op jit(solution)/shard_map/jit(_where)/select_n | solution.py:30
  33.4 6.1 all-to-all-start.1
  40.0 0.7 multiply_reduce_fusion
  41.3 294.9 %all-to-all-done.1 = bf16[16,8,128,512]{3,2,1,0:T(8,128)(2,1)} async-done(((bf16[16,8,128,512]{3,2,1,0:T(8,128)(2,1)}), bf16[16,8,128,512]{3,2,1,0:T(8,128)(2,1)}, u32[]{:S(2)}, u32[]{:S(2)}) %all-to-all-start.1) | async-done | bytes 16777248 | tf_op jit(solution)/shard_map/all_to_all | solution.py:32
  336.2 11.3 %gather_fusion.2 = bf16[64,128,512]{2,1,0:T(8,128)(2,1)} fusion(bf16[128,128,512]{2,1,0:T(8,128)(2,1)} %bitcast.6, s32[1024]{0:T(1024)S(1)} %pad_clamp_fusion.3), kind=kCustom, calls=%fused_computation.2 | custom fusion | bytes 16777472 | tf_op jit(solution)/shard_map/gather | solution.py:56
  347.5 7.2 %broadcast_select_fusion.1 = bf16[2,32,128,512]{3,2,1,0:T(8,128)(2,1)} fusion(bf16[2,32,128,512]{3,2,1,0:T(8,128)(2,1)} %bitcast.85, pred[2,32]{1,0:T(4,128)(4,1)S(1)} %broadcast_in_dim.140), kind=kLoop, calls=%fused_computation.13 | loop fusion | flops 4194304 | bytes 16777280 | tf_op jit(solution)/shard_map/jit(_where)/select_n | solution.py:55
  354.7 7.1 %all-to-all-start.2 = ((bf16[2,32,128,512]{3,2,1,0:T(8,128)(2,1)}), bf16[2,32,128,512]{3,2,1,0:T(8,128)(2,1)}, u32[]{:S(2)}, u32[]{:S(2)}) async-start(bf16[2,32,128,512]{3,2,1,0:T(8,128)(2,1)} %broadcast_select_fusion.1), calls=%async_computation.2 | async-start | bytes 16777216 | tf_op jit(solution)/shard_map/all_to_all | solution.py:58
  362.4 93.0 %all-to-all-done.2 = bf16[2,32,128,512]{3,2,1,0:T(8,128)(2,1)} async-done(((bf16[2,32,128,512]{3,2,1,0:T(8,128)(2,1)}), bf16[2,32,128,512]{3,2,1,0:T(8,128)(2,1)}, u32[]{:S(2)}, u32[]{:S(2)}) %all-to-all-start.2) | async-done | bytes 8388640 | tf_op jit(solution)/shard_map/all_to_all | solution.py:58
  455.3 16.4 %copy.20 = bf16[1,32,128,2,512]{4,3,2,1,0:T(2,128)(2,1)} copy(bf16[1,32,128,2,512]{4,2,1,3,0:T(8,128)(2,1)} %bitcast.11) | data formatting | bytes 16777216 | tf_op jit(solution)/shard_map/all_to_all | solution.py:58
  471.7 14.3 %reshape.447 = bf16[32,128,1024]{2,1,0:T(8,128)(2,1)} reshape(bf16[1,32,128,2,512]{4,3,2,1,0:T(2,128)(2,1)} %copy.20) | data formatting | bytes 16777216 | tf_op jit(solution)/shard_map/reshape | solution.py:65
  486.1 7.3 %add_reduce_fusion = (f32[32,128]{1,0:T(8,128)S(1)}, f32[32,128,512]{2,1,0:T(8,128)S(1)}) fusion(f32[512]{0:T(512)S(1)} %bitcast.89, bf16[32,128,1024]{2,1,0:T(8,128)(2,1)} %reshape.447, bf16[1,512,1024]{2,1,0:T(8,128)(2,1)S(1)} %copy-done.5), kind=kOutput, calls=%fused_computation.14 | convolution fusion | flops 4299157504 | bytes 17844224 | tf_op jit(solution)/shard_map/hrd,cd->hrc/dot_general | solution.py:72
  493.3 4.4 all-gather
  497.8 2.0 exponential_reduce_fusion.1
  499.8 4.4 all-gather.1
  504.2 0.6 gather_fusion.5
  504.9 0.6 gather_fusion.3
  505.5 0.7 bitcast_select_fusion.1
  506.3 69.7 %all-to-all-start.3 = ((f32[16,8,128]{2,1,0:T(8,128)}), f32[16,8,128]{2,1,0:T(8,128)S(1)}, u32[]{:S(2)}, u32[]{:S(2)}) async-start(f32[16,8,128]{2,1,0:T(8,128)} %get-tuple-element.5), calls=%async_computation.3 | async-start | bytes 131072 | tf_op jit(solution)/shard_map/all_to_all | solution.py:86
  576.0 6.9 %all-to-all-done.3 = f32[16,8,128]{2,1,0:T(8,128)S(1)} async-done(((f32[16,8,128]{2,1,0:T(8,128)}), f32[16,8,128]{2,1,0:T(8,128)S(1)}, u32[]{:S(2)}, u32[]{:S(2)}) %all-to-all-start.3) | async-done | bytes 65568 | tf_op jit(solution)/shard_map/all_to_all | solution.py:86
  582.9 3.5 all-to-all-start.4
  587.1 6.1 all-to-all-done.4
  593.9 0.6 gather_fusion.7
  594.5 0.7 bitcast_select_fusion
  595.3 3.7 all-to-all-start.5
  599.0 6.6 %all-to-all-done.5 = f32[16,8,128]{2,1,0:T(8,128)S(1)} async-done(((f32[16,8,128]{2,1,0:T(8,128)}), f32[16,8,128]{2,1,0:T(8,128)S(1)}, u32[]{:S(2)}, u32[]{:S(2)}) %all-to-all-start.5) | async-done | bytes 65568 | tf_op jit(solution)/shard_map/all_to_all | solution.py:111
  606.2 7.4 %fusion = (f32[512]{0:T(512)S(1)}, f32[32,128,512]{2,1,0:T(8,128)S(1)}) fusion(f32[32,128]{1,0:T(8,128)S(1)} %gather_fusion.8, pred[32]{0:T(512)(128)(4,1)S(1)} %dynamic-slice_bitcast_fusion, bf16[32,128,1024]{2,1,0:T(8,128)(2,1)} %reshape.447, bf16[1,512,1024]{2,1,0:T(8,128)(2,1)S(1)} %copy-done.5), kind=kOutput, calls=%fused_computation.15 | convolution fusion | flops 4301258240 | bytes 17844256 | tf_op jit(solution)/shard_map/hrd,cd->hrc/dot_general | solution.py:119
  613.6 1.9 exponential_reduce_fusion
  (54 shorter events, 4.7 us)
Async XLA Ops:
  0.6 10.7 %copy-start = (bf16[8,128,512]{2,1,0:T(8,128)(2,1)S(1)}, bf16[8,128,512]{2,1,0:T(8,128)(2,1)}, u32[]{:S(2)}) copy-start(bf16[8,128,512]{2,1,0:T(8,128)(2,1)} %param.4) | copy-start | bytes 3145732
  3.9 29.5 %all-to-all-start = ((s32[16,1,8]{2,1,0:T(1,128)}), s32[16,1,8]{2,1,0:T(1,128)S(1)}, u32[]{:S(2)}, u32[]{:S(2)}) async-start(s32[16,1,8]{2,1,0:T(1,128)} %bitcast.2), calls=%async_computation | async-start | bytes 16384 | tf_op jit(solution)/shard_map/all_to_all | solution.py:39
  33.4 302.8 %all-to-all-start.1 = ((bf16[16,8,128,512]{3,2,1,0:T(8,128)(2,1)}), bf16[16,8,128,512]{3,2,1,0:T(8,128)(2,1)}, u32[]{:S(2)}, u32[]{:S(2)}) async-start(bf16[16,8,128,512]{3,2,1,0:T(8,128)(2,1)} %broadcast_select_fusion), calls=%async_computation.1 | async-start | bytes 33554432 | tf_op jit(solution)/shard_map/all_to_all | solution.py:32
  354.7 7.1 %copy-start.3 = (s32[8,8]{1,0:T(8,128)S(1)}, s32[8,8]{1,0:T(8,128)}, u32[]{:S(2)}) copy-start(s32[8,8]{1,0:T(8,128)} %param.7) | copy-start | bytes 772
  354.7 100.6 %all-to-all-start.2 = ((bf16[2,32,128,512]{3,2,1,0:T(8,128)(2,1)}), bf16[2,32,128,512]{3,2,1,0:T(8,128)(2,1)}, u32[]{:S(2)}, u32[]{:S(2)}) async-start(bf16[2,32,128,512]{3,2,1,0:T(8,128)(2,1)} %broadcast_select_fusion.1), calls=%async_computation.2 | async-start | bytes 16777216 | tf_op jit(solution)/shard_map/all_to_all | solution.py:58
  471.7 14.4 %copy-start.4 = (f32[1,512]{1,0:T(1,128)S(1)}, f32[1,512]{1,0:T(1,128)}, u32[]{:S(2)}) copy-start(f32[1,512]{1,0:T(1,128)} %param.6) | copy-start | bytes 6148
  471.7 14.4 %copy-start.5 = (bf16[1,512,1024]{2,1,0:T(8,128)(2,1)S(1)}, bf16[1,512,1024]{2,1,0:T(8,128)(2,1)}, u32[]{:S(2)}) copy-start(bf16[1,512,1024]{2,1,0:T(8,128)(2,1)} %param.5) | copy-start | bytes 3145732
  506.3 76.6 %all-to-all-start.3 = ((f32[16,8,128]{2,1,0:T(8,128)}), f32[16,8,128]{2,1,0:T(8,128)S(1)}, u32[]{:S(2)}, u32[]{:S(2)}) async-start(f32[16,8,128]{2,1,0:T(8,128)} %get-tuple-element.5), calls=%async_computation.3 | async-start | bytes 131072 | tf_op jit(solution)/shard_map/all_to_all | solution.py:86
  582.9 10.4 %all-to-all-start.4 = ((f32[16,8,128]{2,1,0:T(8,128)}), f32[16,8,128]{2,1,0:T(8,128)S(1)}, u32[]{:S(2)}, u32[]{:S(2)}) async-start(f32[16,8,128]{2,1,0:T(8,128)} %get-tuple-element.4), calls=%async_computation.4 | async-start | bytes 131072 | tf_op jit(solution)/shard_map/all_to_all | solution.py:93
  593.9 19.7 %copy-start.2 = (f32[8,128]{1,0:T(8,128)}, f32[8,128]{1,0:T(8,128)S(1)}, u32[]{:S(2)}) copy-start(f32[8,128]{1,0:T(8,128)S(1)} %add_negate_fusion) | copy-start | bytes 12292
  595.3 10.4 %all-to-all-start.5 = ((f32[16,8,128]{2,1,0:T(8,128)}), f32[16,8,128]{2,1,0:T(8,128)S(1)}, u32[]{:S(2)}, u32[]{:S(2)}) async-start(f32[16,8,128]{2,1,0:T(8,128)} %bitcast_select_fusion), calls=%async_computation.5 | async-start | bytes 131072 | tf_op jit(solution)/shard_map/all_to_all | solution.py:111
  606.2 9.9 %copy-start.1 = (bf16[8,128,512]{2,1,0:T(8,128)(2,1)S(1)}, bf16[8,128,512]{2,1,0:T(8,128)(2,1)}, u32[]{:S(2)}) copy-start(bf16[8,128,512]{2,1,0:T(8,128)(2,1)} %param.4) | copy-start | bytes 3145732
where the time goes:
time: 617 us; the launch traced here: 616 us
  waiting for transfers between devices  408 us (66%)
  starting transfers between devices  97.4 us (16%)
  local copies, waits for them, and re-layouts  58 us (9%)
  other arithmetic  28.8 us (5%)
  matrix products  14.7 us (2%)
  blocking collectives  8.83 us (1%)
    all_to_all x1, waiting for transfers between devices, body(): lax.all_to_all(outgoing.reshape(groups, capacity, row_count, slice_width)...  295 us
    all_to_all x1, waiting for transfers between devices, body(): lax.all_to_all(sectioned.reshape(owners, bucket_cap, row_count, slice_wid...  93 us
    all_to_all x1, starting transfers between devices, body(): lax.all_to_all(back_peak.reshape(groups, capacity, row_count), 'pts', spl...  69.7 us
    all_to_all x1, local copies, waits for them, and re-layouts, body(): lax.all_to_all(sectioned.reshape(owners, bucket_cap, row_count, slice_wid...  16.4 us
    reshape x1, local copies, waits for them, and re-layouts, body(): resident = resident.reshape(bucket_cap, row_count, slice_width * owners)  14.3 us
    select_n x1, other arithmetic, body(): jnp.where(filled[:, None, None], points[block_of_slot], jnp.zeros((), poi...  14 us
  transfers between devices with their start and end apart: 6, of which 5 were waited for; matrix products, arithmetic and copies ran while one was open for 4% of the time, Pallas kernels for 0%

commit v1 on v0

v1 whole, which is shorter than its diff:
```python
import functools

import jax
import jax.numpy as jnp
from jax import lax
from jax.experimental import pallas as pl
from jax.experimental.pallas import tpu as pltpu
from jax.sharding import Mesh, PartitionSpec as P

LOWEST = -1e30
PLANE = 4


def scores_of(points_ref, protos_ref, k, first, second):
    rows = jnp.concatenate([points_ref[first], points_ref[second]], axis=0)
    return lax.dot_general(
        protos_ref[k], rows, (((1,), (1,)), ((), ())), preferred_element_type=jnp.float32
    )


def row_kernel(order_ref, count_ref, points_ref, protos_ref, coarse_ref, out_ref):
    depth, most, rows = out_ref.shape
    out_ref[...] = jnp.full(out_ref.shape, LOWEST, jnp.float32)
    for k in range(depth):
        count = count_ref[k]

        def step(s, _):
            first = order_ref[k, 2 * s]
            second = order_ref[k, 2 * s + 1]
            shifted = scores_of(points_ref, protos_ref, k, first, second) + coarse_ref[k]
            peak = jnp.max(shifted, axis=0, keepdims=True)
            mass = jnp.sum(jnp.exp(shifted - peak), axis=0, keepdims=True)
            value = peak + jnp.log(mass)
            spare = jnp.where(2 * s + 1 < count, second, most - 1)
            out_ref[k, pl.ds(first, 1)] = value[:, :rows]
            out_ref[k, pl.ds(spare, 1)] = value[:, rows:]
            return 0

        lax.fori_loop(0, (count + 1) // 2, step, 0)


def column_kernel(order_ref, count_ref, points_ref, protos_ref, duals_ref, out_ref, peak_ref, mass_ref):
    depth = out_ref.shape[0]
    for k in range(depth):
        count = count_ref[k]
        peak_ref[...] = jnp.full(peak_ref.shape, LOWEST, jnp.float32)
        mass_ref[...] = jnp.zeros(mass_ref.shape, jnp.float32)

        def step(s, _):
            first = order_ref[k, 2 * s]
            second = order_ref[k, 2 * s + 1]
            scores = scores_of(points_ref, protos_ref, k, first, second)
            after = duals_ref[pl.ds(second, 1)] + jnp.where(2 * s + 1 < count, 0.0, LOWEST)
            arg = scores + jnp.concatenate([duals_ref[pl.ds(first, 1)], after], axis=1)
            old = peak_ref[...]
            new = jnp.maximum(old, arg)
            mass_ref[...] = mass_ref[...] * jnp.exp(old - new) + jnp.exp(arg - new)
            peak_ref[...] = new
            return 0

        lax.fori_loop(0, (count + 1) // 2, step, 0)
        peak = jnp.max(peak_ref[...], axis=1, keepdims=True)
        mass = jnp.sum(mass_ref[...] * jnp.exp(peak_ref[...] - peak), axis=1, keepdims=True)
        value = jnp.where(mass > 0.0, peak + jnp.log(mass), LOWEST)
        out_ref[k] = value.reshape(1, -1)


def lse(x, axis):
    peak = jnp.max(x, axis=axis, keepdims=True)
    return jnp.squeeze(peak + jnp.log(jnp.sum(jnp.exp(x - peak), axis=axis, keepdims=True)), axis)


def body(points, prototypes, coarse_duals, active):
    depth = lax.axis_size("z")
    owners = lax.axis_size("proto")
    plane = lax.axis_size("r")
    blocks, rows, _ = points.shape
    columns = prototypes.shape[1]
    held = blocks * plane

    protos = lax.all_gather(prototypes, "z", axis=0, tiled=True)
    coarse = lax.all_gather(coarse_duals, "z", axis=0, tiled=True)
    wide = lax.all_gather(points, "proto", axis=2, tiled=True)
    wide = lax.all_gather(wide, "r", axis=0, tiled=True)
    targets = lax.all_gather(active, "r", axis=0, tiled=True)

    mine = (jnp.arange(depth, dtype=jnp.int32) * plane + lax.axis_index("r")) * owners + lax.axis_index("proto")
    named = jnp.any(targets[None] == mine[:, None, None], axis=2)
    ids = jnp.arange(held, dtype=jnp.int32)
    place = jnp.sum((named[:, None, :] & (ids[None, :] < ids[:, None])[None]).astype(jnp.int32), axis=2)
    hit = named[:, None, :] & (place[:, None, :] == ids[None, :, None])
    order = jnp.sum(jnp.where(hit, ids[None, None, :], 0), axis=2)
    count = jnp.sum(named.astype(jnp.int32), axis=1)

    smem = pl.BlockSpec(memory_space=pltpu.SMEM)
    vmem = pl.BlockSpec(memory_space=pltpu.VMEM)
    params = pltpu.CompilerParams(vmem_limit_bytes=56 * 1024 * 1024)
    partial = pl.pallas_call(
        row_kernel,
        out_shape=jax.ShapeDtypeStruct((depth, held + 8, rows), jnp.float32),
        in_specs=[smem, smem, vmem, vmem, vmem],
        out_specs=vmem,
        compiler_params=params,
    )(order, count, wide, protos, coarse[:, :, None])
    partial = lse(partial[:, :held], 0)
    partial = lax.all_gather(partial[None], ("r", "proto"), axis=0, tiled=True)
    duals = -lse(partial, 0)
    point_duals = lax.dynamic_slice_in_dim(duals, lax.axis_index("r") * blocks, blocks, 0)
    sums = pl.pallas_call(
        column_kernel,
        out_shape=jax.ShapeDtypeStruct((depth, 1, columns), jnp.float32),
        in_specs=[smem, smem, vmem, vmem, vmem],
        out_specs=vmem,
        scratch_shapes=[
            pltpu.VMEM((columns, 2 * rows), jnp.float32),
            pltpu.VMEM((columns, 2 * rows), jnp.float32),
        ],
        compiler_params=params,
    )(order, count, wide, protos, duals)
    sums = lax.all_to_all(sums[:, 0], "z", split_axis=0, concat_axis=0, tiled=True)
    return point_duals, -lse(sums, 0)[None]


def solution(mesh):
    groups, owners = mesh.shape["pts"], mesh.shape["proto"]
    plane = PLANE if groups % PLANE == 0 else 1
    grid = Mesh(mesh.devices.reshape(groups // plane, plane, owners), ("z", "r", "proto"))
    pts = ("z", "r")
    both = ("z", "r", "proto")
    return jax.shard_map(
        body,
        mesh=grid,
        in_specs=(P(pts, None, "proto"), P(both, None, None), P(both, None), P(pts, None)),
        out_specs=(P(pts, None), P(both, None)),
        check_vma=False,
    )
```

time: 617 us -> 254 us (0.41)
  waiting for transfers between devices: 408 us -> 163 us
  starting transfers between devices: 97.4 us -> 4.79 us
  local copies, waits for them, and re-layouts: 58 us -> 2.65 us
  Pallas kernels: 0 us -> 29.2 us
  blocking collectives: 8.83 us -> 36 us
  other arithmetic: 28.8 us -> 4.67 us
  matrix products: 14.7 us -> 0 us
  between operations: 0.94 us -> 13.8 us
    all_to_all x6 -> x1, waiting for transfers between devices: 408 us -> 4.33 us  [body(): lax.all_to_all(sums[:, 0], 'z', split_axis=0, concat_axis=0, tiled=True)]
    all_gather x0 -> x3, waiting for transfers between devices: none -> 157 us  [the longest x1 62.1 us: body(): protos = lax.all_gather(prototypes, 'z', axis=0, tiled=True)]
    all_to_all x6 -> x1, starting transfers between devices: 97.4 us -> 4.68 us  [body(): lax.all_to_all(sums[:, 0], 'z', split_axis=0, concat_axis=0, tiled=True)]
    pallas_call x0 -> x2, Pallas kernels: none -> 29.2 us  [the longest x1 14.6 us: body(): pl.pallas_call(row_kernel, out_shape=jax.ShapeDtypeStruct((depth, held +...]
    all_gather x2 -> x3, blocking collectives: 8.83 us -> 36 us  [the longest x1 18.8 us: body(): partial = lax.all_gather(partial[None], ('r', 'proto'), axis=0, tiled=True)]
    gather x9 -> x0, local copies, waits for them, and re-layouts: 24.3 us -> none  [the longest x1 11.3 us: body(): arrived[slot_of_bucket]]
    select_n x12 -> x0, other arithmetic: 22.7 us -> none  [the longest x1 14 us: body(): jnp.where(filled[:, None, None], points[block_of_slot], jnp.zeros((), poi...]
    all_to_all x3 -> x0, local copies, waits for them, and re-layouts: 17 us -> none  [the longest x1 16.4 us: body(): lax.all_to_all(sectioned.reshape(owners, bucket_cap, row_count, slice_wid...]
  transfers between devices with their start and end apart: 6 -> 4, of which waited for: 5 -> 4; matrix products, arithmetic and copies ran while one was open for 4% -> 2% of each run, Pallas kernels for 0% -> 0%
where the time goes in v1:
time: 254 us
  waiting for transfers between devices  163 us (64%)
  blocking collectives  36 us (14%)
  Pallas kernels  29.2 us (11%)
  between operations  13.8 us (5%)
  starting transfers between devices  4.79 us (2%)
  other arithmetic  4.67 us (2%)
  local copies, waits for them, and re-layouts  2.65 us (1%)
    all_gather x1, waiting for transfers between devices, body(): protos = lax.all_gather(prototypes, 'z', axis=0, tiled=True)  62.1 us
    all_gather x1, waiting for transfers between devices, body(): wide = lax.all_gather(wide, 'r', axis=0, tiled=True)  58.4 us
    all_gather x1, waiting for transfers between devices, body(): wide = lax.all_gather(points, 'proto', axis=2, tiled=True)  36.7 us
    all_gather x1, blocking collectives, body(): partial = lax.all_gather(partial[None], ('r', 'proto'), axis=0, tiled=True)  18.8 us
    pallas_call x1, Pallas kernels, body(): pl.pallas_call(row_kernel, out_shape=jax.ShapeDtypeStruct((depth, held +...  14.6 us
    pallas_call x1, Pallas kernels, body(): pl.pallas_call(column_kernel, out_shape=jax.ShapeDtypeStruct((depth, 1, c...  14.6 us
    all_gather x1, blocking collectives, body(): coarse = lax.all_gather(coarse_duals, 'z', axis=0, tiled=True)  12 us
    all_gather x1, blocking collectives, body(): targets = lax.all_gather(active, 'r', axis=0, tiled=True)  5.19 us
  transfers between devices with their start and end apart: 4, of which 4 were waited for; matrix products, arithmetic and copies ran while one was open for 2% of the time, Pallas kernels for 0%

profile of v1, /device:TPU:0, one launch (start us, length us, event | category | flops | bytes accessed | tf_op | source)
XLA Modules:
  0.0 254.1 jit_solution(15519388711286858856)
XLA Ops:
  7.2 0.0 copy-start
  7.2 0.0 copy-start.1
  7.2 0.0 all-gather.6.cloned.1.call-start
  7.2 0.7 all-gather.6.cloned.1.call-update
  7.9 0.0 all-gather.10.cloned.1.call-start
  8.0 0.7 all-gather.10.cloned.1.call-update
  8.7 0.0 all-gather.8.cloned.1.call-start
  8.7 36.7 %all-gather.6.cloned.1.call-done = bf16[8,128,1024]{2,1,0:T(8,128)(2,1)} async-done(((bf16[8,128,512]{2,1,0:T(8,128)(2,1)}), bf16[8,128,1024]{2,1,0:T(8,128)(2,1)}) %all-gather.6.cloned.1.call-update) | async-done | bytes 2097168 | tf_op jit(solution)/shard_map/all_gather | solution.py:83
  45.4 0.0 all-gather.8.cloned.1.call-update
  45.4 0.0 copy-done
  45.5 5.2 %all_gather.18 = s32[32,8]{1,0:T(8,128)S(1)} all-gather(s32[8,8]{1,0:T(8,128)S(1)} %copy-done), channel_id=1, replica_groups=mesh['z'=4,'r'=4,'proto'=2] {'r'}, dimensions={0}, use_global_device_ids=true | all-gather | bytes 1280 | tf_op jit(solution)/shard_map/all_gather | solution.py:85
  50.6 0.1 copy.8
  50.7 0.0 copy-done.1
  50.7 12.0 %all-gather.1 = f32[4,1,512]{2,1,0:T(1,128)S(1)} all-gather(f32[1,1,512]{2,1,0:T(1,128)S(1)} %bitcast.11), channel_id=1, replica_groups=mesh['z'=4,'r'=4,'proto'=2] {'z'}, dimensions={0}, use_global_device_ids=true | all-gather | bytes 10240 | tf_op jit(solution)/shard_map/all_gather | solution.py:82
  62.7 1.3 broadcast_in_dim.13.coarse_ref
  64.1 0.1 compare_reduce_fusion
  64.2 0.6 convert_reduce_fusion.1.count_ref
  64.8 0.1 convert_reduce_fusion
  64.9 0.7 select_reduce_fusion.order_ref
  65.7 62.1 %all-gather.10.cloned.1.call-done.protos_ref = bf16[4,512,1024]{2,1,0:T(8,128)(2,1)} async-done(((bf16[1,512,1024]{2,1,0:T(8,128)(2,1)}), bf16[4,512,1024]{2,1,0:T(8,128)(2,1)}) %all-gather.10.cloned.1.call-update) | async-done | bytes 4194320 | tf_op jit(solution)/shard_map/all_gather | solution.py:81
  127.8 58.4 %all-gather.8.cloned.1.call-done.points_ref = bf16[32,128,1024]{2,1,0:T(8,128)(2,1)} async-done(((bf16[8,128,1024]{2,1,0:T(8,128)(2,1)}), bf16[32,128,1024]{2,1,0:T(8,128)(2,1)}) %all-gather.8.cloned.1.call-update) | async-done | bytes 8388624 | tf_op jit(solution)/shard_map/all_gather | solution.py:84
  186.2 14.6 %shard_map.59 = f32[4,40,128]{2,1,0:T(8,128)} custom-call(s32[4,32]{1,0:T(4,128)} %select_reduce_fusion.order_ref, s32[4]{0:T(128)} %convert_reduce_fusion.1.count_ref, bf16[32,128,1024]{2,1,0:T(8,128)(2,1)} %all-gather.8.cloned.1.call-done.points_ref, bf16[4,512,1024]{2,1,0:T(8,128)(2,1)} %all-gather.10.cloned.1.call-done.protos_ref, ...), custom_call_target="tpu_custom_call" | custom-call | tf_op jit(solution)/shard_map/pallas_call | solution.py:98
  200.8 0.8 slice_reduce_fusion
  201.7 0.9 exponential_reduce_fusion.1
  202.6 18.8 %all-gather = f32[256,128]{1,0:T(8,128)S(1)} all-gather(f32[32,128]{1,0:T(8,128)S(1)} %log_add_fusion), channel_id=2, replica_groups=mesh['z'=4,'r'=4,'proto'=2] {'r','proto'}, dimensions={0}, use_global_device_ids=true | all-gather | bytes 147456 | tf_op jit(solution)/shard_map/all_gather | solution.py:106
  221.5 0.6 add_negate_fusion.duals_ref
  222.1 14.6 %shard_map.60 = f32[4,1,512]{2,1,0:T(1,128)} custom-call(s32[4,32]{1,0:T(4,128)} %select_reduce_fusion.order_ref, s32[4]{0:T(128)} %convert_reduce_fusion.1.count_ref, bf16[32,128,1024]{2,1,0:T(8,128)(2,1)} %all-gather.8.cloned.1.call-done.points_ref, bf16[4,512,1024]{2,1,0:T(8,128)(2,1)} %all-gather.10.cloned.1.call-done.protos_ref, ...), custom_call_target="tpu_custom_call" | custom-call | tf_op jit(solution)/shard_map/pallas_call | solution.py:109
  236.7 4.7 %all-to-all-start = ((f32[4,1,512]{2,1,0:T(1,128)}), f32[4,1,512]{2,1,0:T(1,128)S(1)}, u32[]{:S(2)}, u32[]{:S(2)}) async-start(f32[4,1,512]{2,1,0:T(1,128)} %shard_map.60), calls=%async_computation | async-start | bytes 16384 | tf_op jit(solution)/shard_map/all_to_all | solution.py:120
  241.3 1.3 constant_dynamic-slice_fusion
  242.6 4.3 %all-to-all-done = f32[4,1,512]{2,1,0:T(1,128)S(1)} async-done(((f32[4,1,512]{2,1,0:T(1,128)}), f32[4,1,512]{2,1,0:T(1,128)S(1)}, u32[]{:S(2)}, u32[]{:S(2)}) %all-to-all-start) | async-done | bytes 8224 | tf_op jit(solution)/shard_map/all_to_all | solution.py:120
  247.0 0.6 add_negate_fusion.1
  (8 shorter events, 0.1 us)
Async XLA Ops:
  7.2 38.3 %copy-start = (s32[8,8]{1,0:T(8,128)S(1)}, s32[8,8]{1,0:T(8,128)}, u32[]{:S(2)}) copy-start(s32[8,8]{1,0:T(8,128)} %param.7) | copy-start | bytes 772
  7.2 43.5 %copy-start.1 = (f32[1,512]{1,0:T(1,128)S(1)}, f32[1,512]{1,0:T(1,128)}, u32[]{:S(2)}) copy-start(f32[1,512]{1,0:T(1,128)} %param.6) | copy-start | bytes 6148
  7.2 38.2 %all-gather.6.cloned.1.call-start = ((), (), s32[]{:S(2)}) async-start(), calls=%async_computation.1 | async-start | bytes 3145728 | tf_op jit(solution)/shard_map/all_gather | solution.py:83
  7.9 119.9 %all-gather.10.cloned.1.call-start = ((), (), s32[]{:S(2)}) async-start(), calls=%async_computation.3 | async-start | bytes 5242880 | tf_op jit(solution)/shard_map/all_gather | solution.py:81
  8.7 177.5 %all-gather.8.cloned.1.call-start = ((), (), s32[]{:S(2)}) async-start(), calls=%async_computation.2 | async-start | bytes 10485760 | tf_op jit(solution)/shard_map/all_gather | solution.py:84
  236.7 10.3 %all-to-all-start = ((f32[4,1,512]{2,1,0:T(1,128)}), f32[4,1,512]{2,1,0:T(1,128)S(1)}, u32[]{:S(2)}, u32[]{:S(2)}) async-start(f32[4,1,512]{2,1,0:T(1,128)} %shard_map.60), calls=%async_computation | async-start | bytes 16384 | tf_op jit(solution)/shard_map/all_to_all | solution.py:120
Sparse Core Ops, SparseCore 0:
  9.6 35.8 all-gather.5
  47.0 80.7 all-gather.9
  129.4 56.8 all-gather.7

commit v2 on v1

--- a/solution.py
+++ b/solution.py
@@ -9,10 +9,16 @@
 
 LOWEST = -1e30
 PLANE = 4
+MESH = pl.DeviceIdType.MESH
+
+
+def block_of(points_ref, i):
+    _, owners, blocks, _, _ = points_ref.shape
+    return jnp.concatenate([points_ref[i // blocks, o, i % blocks] for o in range(owners)], axis=1)
 
 
 def scores_of(points_ref, protos_ref, k, first, second):
-    rows = jnp.concatenate([points_ref[first], points_ref[second]], axis=0)
+    rows = jnp.concatenate([block_of(points_ref, first), block_of(points_ref, second)], axis=0)
     return lax.dot_general(
         protos_ref[k], rows, (((1,), (1,)), ((), ())), preferred_element_type=jnp.float32
     )
@@ -23,11 +29,12 @@
     out_ref[...] = jnp.full(out_ref.shape, LOWEST, jnp.float32)
     for k in range(depth):
         count = count_ref[k]
+        coarse = coarse_ref[k].reshape(-1, 1)
 
         def step(s, _):
             first = order_ref[k, 2 * s]
             second = order_ref[k, 2 * s + 1]
-            shifted = scores_of(points_ref, protos_ref, k, first, second) + coarse_ref[k]
+            shifted = scores_of(points_ref, protos_ref, k, first, second) + coarse
             peak = jnp.max(shifted, axis=0, keepdims=True)
             mass = jnp.sum(jnp.exp(shifted - peak), axis=0, keepdims=True)
             value = peak + jnp.log(mass)
@@ -70,30 +77,319 @@
     return jnp.squeeze(peak + jnp.log(jnp.sum(jnp.exp(x - peak), axis=axis, keepdims=True)), axis)
 
 
+def place(z, r, o):
+    return {"z": z, "r": r, "proto": o}
+
+
+def greet(partners, count):
+    barrier = pltpu.get_barrier_semaphore()
+    for where, there in partners:
+        if where is None:
+            pl.semaphore_signal(barrier, inc=1, device_id=there, device_id_type=MESH)
+        else:
+
+            @pl.when(where)
+            def _():
+                pl.semaphore_signal(barrier, inc=1, device_id=there, device_id_type=MESH)
+
+    pl.semaphore_wait(barrier, count)
+
+
+def gather_kernel(
+    sizes,
+    points_ref,
+    protos_ref,
+    coarse_ref,
+    active_ref,
+    wide_ref,
+    blocks_ref,
+    duals_ref,
+    targets_ref,
+    local_sem,
+    up_send,
+    up_recv,
+    down_send,
+    down_recv,
+    point_send,
+    point_recv,
+    hop_send,
+    hop_recv,
+):
+    depth, plane, owners = sizes
+    halves = 2 if plane % 2 == 0 else 1
+    wings = plane // halves
+    z, r, o = lax.axis_index("z"), lax.axis_index("r"), lax.axis_index("proto")
+    a, c = r // halves, r % halves
+
+    def shifted(da, do):
+        return lax.rem(a + da + wings, wings) * halves, lax.rem(o + do + owners, owners)
+
+    moves = [(da, do) for da in range(wings) for do in range(owners) if da or do]
+    moves.sort(key=lambda m: (m[0] > 0 and m[1] > 0, m[0] > 0))
+    twin = place(z, a * halves + (1 - c), o)
+    partners = [(z + 1 < depth, place(z + 1, r, o)), (z > 0, place(z - 1, r, o))]
+    for da, do in moves:
+        base, there = shifted(da, do)
+        partners.append((None, place(z, base + c, there)))
+    if halves == 2:
+        partners.append((None, twin))
+    greet(partners, len(partners) - 2 + (z + 1 < depth).astype(jnp.int32) + (z > 0).astype(jnp.int32))
+
+    def chain(t, up):
+        slot = z - t if up else z + t
+        send, recv = (up_send, up_recv) if up else (down_send, down_recv)
+        there = place(z + 1 if up else z - 1, r, o)
+        return [
+            pltpu.make_async_remote_copy(
+                src_ref=own if t == 0 else whole.at[pl.ds(slot, 1)],
+                dst_ref=whole.at[pl.ds(slot, 1)],
+                send_sem=send.at[t, n],
+                recv_sem=recv.at[t, n],
+                device_id=there,
+                device_id_type=MESH,
+            )
+            for n, (own, whole) in enumerate([(protos_ref, blocks_ref), (coarse_ref, duals_ref)])
+        ]
+
+    def arriving(t, up):
+        slot = z - 1 - t if up else z + 1 + t
+        recv = up_recv if up else down_recv
+        return [
+            pltpu.make_async_remote_copy(
+                src_ref=whole.at[pl.ds(slot, 1)],
+                dst_ref=whole.at[pl.ds(slot, 1)],
+                send_sem=recv.at[t, n],
+                recv_sem=recv.at[t, n],
+                device_id=place(z, r, o),
+                device_id_type=MESH,
+            )
+            for n, whole in enumerate([blocks_ref, duals_ref])
+        ]
+
+    def sends(t, up):
+        return (z - t >= 0) & (z + 1 < depth) if up else (z + t < depth) & (z > 0)
+
+    def receives(t, up):
+        return z - 1 - t >= 0 if up else z + 1 + t < depth
+
+    def start_chain(t):
+        for up in (True, False):
+
+            @pl.when(sends(t, up))
+            def _():
+                for copy in chain(t, up):
+                    copy.start()
+
+    def wait_chain(t):
+        for up in (True, False):
+
+            @pl.when(receives(t, up))
+            def _():
+                for copy in arriving(t, up):
+                    copy.wait_recv()
+
+    def pair(own, sr, so, there, send, recv, n, tags):
+        copies = [
+            pltpu.make_async_remote_copy(
+                src_ref=points_ref if own else wide_ref.at[sr, so],
+                dst_ref=wide_ref.at[sr, so],
+                send_sem=send.at[n, 0],
+                recv_sem=recv.at[n, 0],
+                device_id=there,
+                device_id_type=MESH,
+            )
+        ]
+        if tags:
+            copies.append(
+                pltpu.make_async_remote_copy(
+                    src_ref=active_ref if own else targets_ref.at[sr],
+                    dst_ref=targets_ref.at[sr],
+                    send_sem=send.at[n, 1],
+                    recv_sem=recv.at[n, 1],
+                    device_id=there,
+                    device_id_type=MESH,
+                )
+            )
+        return copies
+
+    local = [
+        pltpu.make_async_copy(protos_ref, blocks_ref.at[pl.ds(z, 1)], local_sem.at[0]),
+        pltpu.make_async_copy(coarse_ref, duals_ref.at[pl.ds(z, 1)], local_sem.at[1]),
+        pltpu.make_async_copy(points_ref, wide_ref.at[r, o], local_sem.at[2]),
+        pltpu.make_async_copy(active_ref, targets_ref.at[r], local_sem.at[3]),
+    ]
+    start_chain(0)
+    outgoing = []
+    for n, (da, do) in enumerate(moves):
+        base, there = shifted(da, do)
+        copies = pair(True, r, o, place(z, base + c, there), point_send, point_recv, n, do == 0)
+        for copy in copies:
+            copy.start()
+        outgoing += copies
+    spare = len(moves)
+    if halves == 2:
+        copies = pair(True, r, o, twin, hop_send, hop_recv, spare, True)
+        for copy in copies:
+            copy.start()
+        outgoing += copies
+    for copy in local:
+        copy.start()
+
+    def pass_on(n):
+        da, do = moves[n]
+        base, from_o = shifted(-da, -do)
+        copies = pair(False, base + c, from_o, twin, point_send, point_recv, n, do == 0)
+        for copy in copies:
+            copy.wait_recv()
+        if halves == 2:
+            copies = pair(False, base + c, from_o, twin, hop_send, hop_recv, n, do == 0)
+            for copy in copies:
+                copy.start()
+            outgoing.extend(copies)
+
+    steps = max(depth - 1, 1)
+    share = -(-len(moves) // steps)
+    done = 0
+    for t in range(steps):
+        if t < depth - 1:
+            wait_chain(t)
+            if t + 1 < depth - 1:
+                start_chain(t + 1)
+        for n in range(done, min(done + share, len(moves))):
+            pass_on(n)
+        done = min(done + share, len(moves))
+    if halves == 2:
+        for n, (da, do) in enumerate(moves + [(0, 0)]):
+            base, from_o = shifted(-da, -do)
+            for copy in pair(False, base + 1 - c, from_o, twin, hop_send, hop_recv, n, do == 0):
+                copy.wait_recv()
+    for copy in outgoing:
+        copy.wait_send()
+    for t in range(depth - 1):
+        for up in (True, False):
+
+            @pl.when(sends(t, up))
+            def _():
+                for copy in chain(t, up):
+                    copy.wait_send()
+
+    for copy in local:
+        copy.wait()
+
+
+def plane_kernel(sizes, part_ref, out_ref, all_ref, send_sem, recv_sem):
+    depth, plane, owners = sizes
+    z, r, o = lax.axis_index("z"), lax.axis_index("r"), lax.axis_index("proto")
+    me = r * owners + o
+    held = part_ref.shape[1]
+    moves = [(dr, do) for dr in range(plane) for do in range(owners) if dr or do]
+
+    def spot(dr, do):
+        return lax.rem(r + dr + plane, plane), lax.rem(o + do + owners, owners)
+
+    greet([(None, place(z, *spot(*move))) for move in moves], len(moves))
+    all_ref[me] = lse(part_ref[...], 0)
+    copies = [
+        pltpu.make_async_remote_copy(
+            src_ref=all_ref.at[me],
+            dst_ref=all_ref.at[me],
+            send_sem=send_sem.at[n],
+            recv_sem=recv_sem.at[n],
+            device_id=place(z, *spot(*move)),
+            device_id_type=MESH,
+        )
+        for n, move in enumerate(moves)
+    ]
+    for copy in copies:
+        copy.start()
+    for n, (dr, do) in enumerate(moves):
+        sr, so = spot(-dr, -do)
+        slot = all_ref.at[sr * owners + so]
+        pltpu.make_async_remote_copy(
+            src_ref=slot,
+            dst_ref=slot,
+            send_sem=send_sem.at[n],
+            recv_sem=recv_sem.at[n],
+            device_id=place(z, sr, so),
+            device_id_type=MESH,
+        ).wait_recv()
+    out_ref[...] = -lse(all_ref[...], 0)
+    for copy in copies:
+        copy.wait_send()
+
+
+def line_kernel(sizes, part_ref, out_ref, all_ref, send_sem, recv_sem):
+    depth, plane, owners = sizes
+    z, r, o = lax.axis_index("z"), lax.axis_index("r"), lax.axis_index("proto")
+    greet([(None, place(lax.rem(z + d, depth), r, o)) for d in range(1, depth)], depth - 1)
+    all_ref[z] = part_ref[z]
+    copies = []
+    for d in range(1, depth):
+        there = lax.rem(z + d, depth)
+        copies.append(
+            pltpu.make_async_remote_copy(
+                src_ref=part_ref.at[there],
+                dst_ref=all_ref.at[z],
+                send_sem=send_sem.at[d],
+                recv_sem=recv_sem.at[d],
+                device_id=place(there, r, o),
+                device_id_type=MESH,
+            )
+        )
+    for copy in copies:
+        copy.start()
+    for d in range(1, depth):
+        slot = all_ref.at[lax.rem(z + depth - d, depth)]
+        pltpu.make_async_remote_copy(
+            src_ref=slot,
+            dst_ref=slot,
+            send_sem=send_sem.at[d],
+            recv_sem=recv_sem.at[d],
+            device_id=place(lax.rem(z + depth - d, depth), r, o),
+            device_id_type=MESH,
+        ).wait_recv()
+    out_ref[...] = -lse(all_ref[...], 0)
+    for copy in copies:
+        copy.wait_send()
+
+
 def body(points, prototypes, coarse_duals, active):
     depth = lax.axis_size("z")
     owners = lax.axis_size("proto")
     plane = lax.axis_size("r")
-    blocks, rows, _ = points.shape
-    columns = prototypes.shape[1]
+    sizes = (depth, plane, owners)
+    blocks, rows, width = points.shape
+    columns, features = prototypes.shape[1:]
     held = blocks * plane
-
-    protos = lax.all_gather(prototypes, "z", axis=0, tiled=True)
-    coarse = lax.all_gather(coarse_duals, "z", axis=0, tiled=True)
-    wide = lax.all_gather(points, "proto", axis=2, tiled=True)
-    wide = lax.all_gather(wide, "r", axis=0, tiled=True)
-    targets = lax.all_gather(active, "r", axis=0, tiled=True)
+    smem = pl.BlockSpec(memory_space=pltpu.SMEM)
+    vmem = pl.BlockSpec(memory_space=pltpu.VMEM)
+    anywhere = pl.BlockSpec(memory_space=pl.ANY)
+
+    dma = pltpu.SemaphoreType.DMA
+    hops = plane * owners
+    wide, protos, coarse, targets = pl.pallas_call(
+        functools.partial(gather_kernel, sizes),
+        out_shape=(
+            jax.ShapeDtypeStruct((plane, owners, blocks, rows, width), points.dtype),
+            jax.ShapeDtypeStruct((depth, columns, features), prototypes.dtype),
+            jax.ShapeDtypeStruct((depth, 1, columns), jnp.float32),
+            jax.ShapeDtypeStruct((plane,) + active.shape, active.dtype),
+        ),
+        in_specs=[anywhere] * 4,
+        out_specs=(anywhere,) * 4,
+        scratch_shapes=[dma((4,))] + [dma((depth, 2))] * 4 + [dma((hops, 2))] * 4,
+        compiler_params=pltpu.CompilerParams(collective_id=0, has_side_effects=True),
+    )(points, prototypes, coarse_duals[None], active)
+    targets = targets.reshape(held, active.shape[1])
 
     mine = (jnp.arange(depth, dtype=jnp.int32) * plane + lax.axis_index("r")) * owners + lax.axis_index("proto")
     named = jnp.any(targets[None] == mine[:, None, None], axis=2)
     ids = jnp.arange(held, dtype=jnp.int32)
-    place = jnp.sum((named[:, None, :] & (ids[None, :] < ids[:, None])[None]).astype(jnp.int32), axis=2)
-    hit = named[:, None, :] & (place[:, None, :] == ids[None, :, None])
+    spot = jnp.sum((named[:, None, :] & (ids[None, :] < ids[:, None])[None]).astype(jnp.int32), axis=2)
+    hit = named[:, None, :] & (spot[:, None, :] == ids[None, :, None])
     order = jnp.sum(jnp.where(hit, ids[None, None, :], 0), axis=2)
     count = jnp.sum(named.astype(jnp.int32), axis=1)
 
-    smem = pl.BlockSpec(memory_space=pltpu.SMEM)
-    vmem = pl.BlockSpec(memory_space=pltpu.VMEM)
     params = pltpu.CompilerParams(vmem_limit_bytes=56 * 1024 * 1024)
     partial = pl.pallas_call(
         row_kernel,
@@ -101,10 +397,15 @@
         in_specs=[smem, smem, vmem, vmem, vmem],
         out_specs=vmem,
         compiler_params=params,
-    )(order, count, wide, protos, coarse[:, :, None])
-    partial = lse(partial[:, :held], 0)
-    partial = lax.all_gather(partial[None], ("r", "proto"), axis=0, tiled=True)
-    duals = -lse(partial, 0)
+    )(order, count, wide, protos, coarse)
+    duals = pl.pallas_call(
+        functools.partial(plane_kernel, sizes),
+        out_shape=jax.ShapeDtypeStruct((held + 8, rows), jnp.float32),
+        in_specs=[vmem],
+        out_specs=vmem,
+        scratch_shapes=[pltpu.VMEM((hops, held + 8, rows), jnp.float32), dma((hops,)), dma((hops,))],
+        compiler_params=pltpu.CompilerParams(collective_id=1, has_side_effects=True),
+    )(partial)
     point_duals = lax.dynamic_slice_in_dim(duals, lax.axis_index("r") * blocks, blocks, 0)
     sums = pl.pallas_call(
         column_kernel,
@@ -117,8 +418,15 @@
         ],
         compiler_params=params,
     )(order, count, wide, protos, duals)
-    sums = lax.all_to_all(sums[:, 0], "z", split_axis=0, concat_axis=0, tiled=True)
-    return point_duals, -lse(sums, 0)[None]
+    new_duals = pl.pallas_call(
+        functools.partial(line_kernel, sizes),
+        out_shape=jax.ShapeDtypeStruct((1, columns), jnp.float32),
+        in_specs=[vmem],
+        out_specs=vmem,
+        scratch_shapes=[pltpu.VMEM((depth, 1, columns), jnp.float32), dma((depth,)), dma((depth,))],
+        compiler_params=pltpu.CompilerParams(collective_id=2, has_side_effects=True),
+    )(sums)
+    return point_duals, new_duals
 
 
 def solution(mesh):

time: 254 us -> 135 us (0.53)
  waiting for transfers between devices: 163 us -> 0 us
  Pallas kernels: 29.2 us -> 128 us
  blocking collectives: 36 us -> 0 us
  between operations: 13.8 us -> 0.68 us
  starting transfers between devices: 4.79 us -> 0 us
  other arithmetic: 4.67 us -> 1.62 us
    all_gather x3 -> x0, waiting for transfers between devices: 157 us -> none  [the longest x1 62.1 us: body(): protos = lax.all_gather(prototypes, 'z', axis=0, tiled=True)]
    pallas_call x0 -> x3, Pallas kernels: none -> 93.9 us  [the longest x1 80.1 us: body(): pl.pallas_call(functools.partial(gather_kernel, sizes), out_shape=(jax.Sh...]
    all_gather x3 -> x0, blocking collectives: 36 us -> none  [the longest x1 18.8 us: body(): partial = lax.all_gather(partial[None], ('r', 'proto'), axis=0, tiled=True)]
    all_to_all x1 -> x0, starting transfers between devices: 4.68 us -> none  [body(): lax.all_to_all(sums[:, 0], 'z', split_axis=0, concat_axis=0, tiled=True)]
    all_to_all x1 -> x0, waiting for transfers between devices: 4.33 us -> none  [body(): lax.all_to_all(sums[:, 0], 'z', split_axis=0, concat_axis=0, tiled=True)]
    pallas_call x1, Pallas kernels: 14.6 us -> 17.4 us  [body(): pl.pallas_call(row_kernel, out_shape=jax.ShapeDtypeStruct((depth, held +...]
  transfers between devices with their start and end apart: 4 -> 0, of which waited for: 4 -> 0; matrix products, arithmetic and copies ran while one was open for 2% -> 0% of each run, Pallas kernels for 0% -> 0%
where the time goes in v2:
time: 135 us; the launch traced here: 134 us
  Pallas kernels  128 us (95%)
  local copies, waits for them, and re-layouts  3.32 us (2%)
  other arithmetic  1.62 us (1%)
    pallas_call x1, Pallas kernels, body(): pl.pallas_call(functools.partial(gather_kernel, sizes), out_shape=(jax.Sh...  80.1 us
    pallas_call x1, Pallas kernels, body(): pl.pallas_call(row_kernel, out_shape=jax.ShapeDtypeStruct((depth, held +...  17.4 us
    pallas_call x1, Pallas kernels, body(): pl.pallas_call(column_kernel, out_shape=jax.ShapeDtypeStruct((depth, 1, c...  16.8 us
    pallas_call x1, Pallas kernels, body(): pl.pallas_call(functools.partial(plane_kernel, sizes), out_shape=jax.Shap...  6.96 us
    pallas_call x1, Pallas kernels, body(): pl.pallas_call(functools.partial(line_kernel, sizes), out_shape=jax.Shape...  6.79 us

profile of v2, /device:TPU:0, one launch (start us, length us, event | category | flops | bytes accessed | tf_op | source)
XLA Modules:
  0.0 133.7 jit_solution(4789381356572827910)
XLA Ops:
  0.7 80.1 %shard_map.59 = (bf16[4,2,8,128,512]{4,3,2,1,0:T(8,128)(2,1)}, bf16[4,512,1024]{2,1,0:T(8,128)(2,1)}, f32[4,1,512]{2,1,0:T(1,128)}, s32[4,8,8]{2,1,0:T(8,128)}) custom-call(bf16[8,128,512]{2,1,0:T(8,128)(2,1)} %points_ref.1, bf16[1,512,1024]{2,1,0:T(8,128)(2,1)} %protos_ref.1, f32[1,1,512]{2,1,0:T(1,128)} %bitcast.3, s32[8,8]{1,0:T(8,128)} %active_ref.1), custom_call_target="tpu_custom_call" | custom-call | tf_op jit(solution)/shard_map/pallas_call | solution.py:370
  80.8 0.8 copy.6
  81.6 0.1 compare_reduce_fusion
  81.7 0.2 convert_reduce_fusion
  81.8 0.7 select_reduce_fusion.order_ref
  82.6 0.6 convert_reduce_fusion.1.count_ref
  83.2 17.4 %shard_map.60.part_ref = f32[4,40,128]{2,1,0:T(8,128)} custom-call(s32[4,32]{1,0:T(4,128)} %select_reduce_fusion.order_ref, s32[4]{0:T(128)} %convert_reduce_fusion.1.count_ref, bf16[4,2,8,128,512]{4,3,2,1,0:T(8,128)(2,1)} %get-tuple-element.7.points_ref, bf16[4,512,1024]{2,1,0:T(8,128)(2,1)} %get-tuple-element.8.protos_ref, ...), custom_call_target="tpu_custom_call" | custom-call | tf_op jit(solution)/shard_map/pallas_call | solution.py:394
  100.5 7.0 %shard_map.61.duals_ref = f32[40,128]{1,0:T(8,128)} custom-call(f32[4,40,128]{2,1,0:T(8,128)} %shard_map.60.part_ref), custom_call_target="tpu_custom_call" | custom-call | tf_op jit(solution)/shard_map/pallas_call | solution.py:401
  107.5 16.8 %shard_map.62.part_ref = f32[4,1,512]{2,1,0:T(1,128)} custom-call(s32[4,32]{1,0:T(4,128)} %select_reduce_fusion.order_ref, s32[4]{0:T(128)} %convert_reduce_fusion.1.count_ref, bf16[4,2,8,128,512]{4,3,2,1,0:T(8,128)(2,1)} %get-tuple-element.7.points_ref, bf16[4,512,1024]{2,1,0:T(8,128)(2,1)} %get-tuple-element.8.protos_ref, f32[40,128]{1,0:T(8,128)} %shard_map.61.duals_ref), custom_call_target="tpu_custom_call" | custom-call | tf_op jit(solution)/shard_map/pallas_call | solution.py:410
  124.3 1.3 constant_dynamic-slice_fusion
  125.6 6.8 %shard_map.63 = f32[1,512]{1,0:T(1,128)} custom-call(f32[4,1,512]{2,1,0:T(1,128)} %shard_map.62.part_ref), custom_call_target="tpu_custom_call" | custom-call | tf_op jit(solution)/shard_map/pallas_call | solution.py:421
  132.4 1.3 copy.8
  (2 shorter events, 0.0 us)

commit v3 on v2

v3 whole, which is shorter than its diff:
```python
import functools

import jax
import jax.numpy as jnp
from jax import lax
from jax.experimental import pallas as pl
from jax.experimental.pallas import tpu as pltpu
from jax.sharding import Mesh, PartitionSpec as P

LOWEST = -1e30
PLANE = 4
PIECES = 2
KEPT_MOST = 32 * 1024 * 1024
VMEM_MOST = 60 * 1024 * 1024
MESH = pl.DeviceIdType.MESH


def block_of(points_ref, i):
    _, owners, blocks, _, _ = points_ref.shape
    return jnp.concatenate([points_ref[i // blocks, o, i % blocks] for o in range(owners)], axis=1)


def scores_of(points_ref, protos_ref, k, s):
    rows = jnp.concatenate([block_of(points_ref, 2 * s), block_of(points_ref, 2 * s + 1)], axis=0)
    return lax.dot_general(
        protos_ref[k], rows, (((1,), (1,)), ((), ())), preferred_element_type=jnp.float32
    )


def beside(ref, s):
    return jnp.concatenate([ref[pl.ds(2 * s, 1)], ref[pl.ds(2 * s + 1, 1)]], axis=1)


def lse(x, axis):
    peak = jnp.max(x, axis=axis, keepdims=True)
    return jnp.squeeze(peak + jnp.log(jnp.sum(jnp.exp(x - peak), axis=axis, keepdims=True)), axis)


def place(z, r, o):
    return {"z": z, "r": r, "proto": o}


def greet(partners):
    barrier = pltpu.get_barrier_semaphore()
    for there in partners:
        pl.semaphore_signal(barrier, inc=1, device_id=there, device_id_type=MESH)
    pl.semaphore_wait(barrier, len(partners))


def fused_kernel(
    sizes,
    keep,
    points_ref,
    protos_ref,
    coarse_ref,
    active_ref,
    point_out,
    proto_out,
    wide_ref,
    blocks_ref,
    duals_ref,
    targets_ref,
    scores_ref,
    part_ref,
    all_ref,
    bias_ref,
    column_ref,
    line_ref,
    total_ref,
    work_ref,
    local_sem,
    up_send,
    up_recv,
    down_send,
    down_recv,
    point_send,
    point_recv,
    hop_send,
    hop_recv,
    plane_send,
    plane_recv,
    line_send,
    line_recv,
):
    depth, plane, owners = sizes
    halves = 2 if plane % 2 == 0 else 1
    wings = plane // halves
    z, r, o = lax.axis_index("z"), lax.axis_index("r"), lax.axis_index("proto")
    a, c = r // halves, r % halves

    def shifted(da, do):
        return lax.rem(a + da + wings, wings) * halves, lax.rem(o + do + owners, owners)

    moves = [(da, do) for da in range(wings) for do in range(owners) if da or do]
    moves.sort(key=lambda m: (m[0] > 0 and m[1] > 0, m[0] > 0))
    twin = place(z, a * halves + (1 - c), o)
    around = [(dr, do) for dr in range(plane) for do in range(owners) if dr or do]

    def spot(dr, do):
        return lax.rem(r + dr + plane, plane), lax.rem(o + do + owners, owners)

    partners = [place(z, *spot(*move)) for move in around]
    partners += [place(lax.rem(z + d, depth), r, o) for d in range(1, depth)]
    greet(partners)

    piece = blocks_ref.shape[1] // PIECES

    def parts(slot, n):
        cut = pl.ds(n * piece, piece)
        pairs = [(protos_ref.at[:, cut], blocks_ref.at[pl.ds(slot, 1), cut])]
        if n == 0:
            pairs.append((coarse_ref, duals_ref.at[pl.ds(slot, 1)]))
        return pairs

    def chain(t, up, n):
        slot = z - t if up else z + t
        send, recv = (up_send, up_recv) if up else (down_send, down_recv)
        return [
            pltpu.make_async_remote_copy(
                src_ref=own if t == 0 else whole,
                dst_ref=whole,
                send_sem=send.at[t, n + PIECES * m],
                recv_sem=recv.at[t, n + PIECES * m],
                device_id=place(z + 1 if up else z - 1, r, o),
                device_id_type=MESH,
            )
            for m, (own, whole) in enumerate(parts(slot, n))
        ]

    def arriving(t, up, n):
        slot = z - 1 - t if up else z + 1 + t
        recv = up_recv if up else down_recv
        return [
            pltpu.make_async_remote_copy(
                src_ref=whole,
                dst_ref=whole,
                send_sem=recv.at[t, n + PIECES * m],
                recv_sem=recv.at[t, n + PIECES * m],
                device_id=place(z, r, o),
                device_id_type=MESH,
            )
            for m, (_, whole) in enumerate(parts(slot, n))
        ]

    def sends(t, up):
        return (z - t >= 0) & (z + 1 < depth) if up else (z + t < depth) & (z > 0)

    def receives(t, up):
        return z - 1 - t >= 0 if up else z + 1 + t < depth

    def start_chain(t, n):
        for up in (True, False):

            @pl.when(sends(t, up))
            def _():
                for copy in chain(t, up, n):
                    copy.start()

    def wait_chain(t, n):
        for up in (True, False):

            @pl.when(receives(t, up))
            def _():
                for copy in arriving(t, up, n):
                    copy.wait_recv()

    def pair(own, sr, so, there, send, recv, n, tags):
        copies = [
            pltpu.make_async_remote_copy(
                src_ref=points_ref if own else wide_ref.at[sr, so],
                dst_ref=wide_ref.at[sr, so],
                send_sem=send.at[n, 0],
                recv_sem=recv.at[n, 0],
                device_id=there,
                device_id_type=MESH,
            )
        ]
        if tags:
            copies.append(
                pltpu.make_async_remote_copy(
                    src_ref=active_ref if own else targets_ref.at[sr],
                    dst_ref=targets_ref.at[sr],
                    send_sem=send.at[n, 1],
                    recv_sem=recv.at[n, 1],
                    device_id=there,
                    device_id_type=MESH,
                )
            )
        return copies

    local = [
        pltpu.make_async_copy(protos_ref, blocks_ref.at[pl.ds(z, 1)], local_sem.at[0]),
        pltpu.make_async_copy(coarse_ref, duals_ref.at[pl.ds(z, 1)], local_sem.at[1]),
        pltpu.make_async_copy(points_ref, wide_ref.at[r, o], local_sem.at[2]),
        pltpu.make_async_copy(active_ref, targets_ref.at[r], local_sem.at[3]),
    ]
    for n in range(PIECES):
        start_chain(0, n)
    outgoing = []
    for n, (da, do) in enumerate(moves):
        base, there = shifted(da, do)
        copies = pair(True, r, o, place(z, base + c, there), point_send, point_recv, n, do == 0)
        for copy in copies:
            copy.start()
        outgoing += copies
    spare = len(moves)
    if halves == 2:
        copies = pair(True, r, o, twin, hop_send, hop_recv, spare, True)
        for copy in copies:
            copy.start()
        outgoing += copies
    for copy in local:
        copy.start()

    def pass_on(n):
        da, do = moves[n]
        base, from_o = shifted(-da, -do)
        copies = pair(False, base + c, from_o, twin, point_send, point_recv, n, do == 0)
        for copy in copies:
            copy.wait_recv()
        if halves == 2:
            copies = pair(False, base + c, from_o, twin, hop_send, hop_recv, n, do == 0)
            for copy in copies:
                copy.start()
            outgoing.extend(copies)

    def settle_points():
        for n in range(len(moves)):
            pass_on(n)
        if halves == 2:
            for n, (da, do) in enumerate(moves + [(0, 0)]):
                base, from_o = shifted(-da, -do)
                for copy in pair(False, base + 1 - c, from_o, twin, hop_send, hop_recv, n, do == 0):
                    copy.wait_recv()
        for copy in local:
            copy.wait()

    held, rows = all_ref.shape[1:]
    columns = blocks_ref.shape[1]
    doubles = held // 2

    def named(k):
        block = (k * plane + r) * owners + o
        tags = targets_ref[...].reshape(held, targets_ref.shape[2])
        return jnp.max(jnp.where(tags == block, 1.0, 0.0), axis=1, keepdims=True) > 0.0

    def score(k):
        coarse = duals_ref[k].reshape(-1, 1)

        def step(s, _):
            found = scores_of(wide_ref, blocks_ref, k, s)
            if keep:
                scores_ref[k, s] = found
            given = found + coarse
            peak = jnp.max(given, axis=0, keepdims=True)
            value = peak + jnp.log(jnp.sum(jnp.exp(given - peak), axis=0, keepdims=True))
            part_ref[k, pl.ds(2 * s, 1)] = value[:, :rows]
            part_ref[k, pl.ds(2 * s + 1, 1)] = value[:, rows:]
            return 0

        lax.fori_loop(0, doubles, step, 0)
        part_ref[k] = jnp.where(named(k), part_ref[k], LOWEST)

    def score_step(t):
        if t < 0:
            score(z)
            return

        def side(n, _):
            slot = z + (1 + t) * (2 * n - 1)

            @pl.when((slot >= 0) & (slot < depth))
            def _():
                score(slot)

            return 0

        lax.fori_loop(0, 2, side, 0)

    todo = list(range(-1, depth - 1))
    settled = False
    for t in range(depth - 1):
        for n in range(PIECES):
            wait_chain(t, n)
            if t + 1 < depth - 1:
                start_chain(t + 1, n)
            if t >= min(1, depth - 2):
                if not settled:
                    settle_points()
                    settled = True
                limit = t - 1 if n < PIECES - 1 else t
                if todo and todo[0] <= limit:
                    score_step(todo.pop(0))
    if not settled:
        settle_points()
    for t in todo:
        score_step(t)

    me = r * owners + o
    all_ref[me] = lse(part_ref[...], 0)
    for n, move in enumerate(around):
        copy = pltpu.make_async_remote_copy(
            src_ref=all_ref.at[me],
            dst_ref=all_ref.at[me],
            send_sem=plane_send.at[n],
            recv_sem=plane_recv.at[n],
            device_id=place(z, *spot(*move)),
            device_id_type=MESH,
        )
        copy.start()
        outgoing.append(copy)
    for n, (dr, do) in enumerate(around):
        sr, so = spot(-dr, -do)
        slot = all_ref.at[sr * owners + so]
        pltpu.make_async_remote_copy(
            src_ref=slot,
            dst_ref=slot,
            send_sem=plane_send.at[n],
            recv_sem=plane_recv.at[n],
            device_id=place(z, sr, so),
            device_id_type=MESH,
        ).wait_recv()
    found = -lse(all_ref[...], 0)
    work_ref[...] = found
    count = points_ref.shape[0]
    point_out[...] = work_ref[pl.ds(pl.multiple_of(r * count, count), count)]

    strip = 64

    def column(k):
        bias_ref[...] = jnp.where(named(k), work_ref[...], LOWEST)

        def over(n, _):
            cut = pl.ds(pl.multiple_of(n * strip, strip), strip)
            peak = jnp.full((strip, 2 * rows), LOWEST, jnp.float32)
            for s in range(doubles):
                peak = jnp.maximum(peak, scores_ref[k, s, cut] + beside(bias_ref, s))
            peak = jnp.max(peak, axis=1, keepdims=True)
            mass = jnp.zeros((strip, 2 * rows), jnp.float32)
            for s in range(doubles):
                mass = mass + jnp.exp(scores_ref[k, s, cut] + beside(bias_ref, s) - peak)
            column_ref[cut] = peak + jnp.log(jnp.sum(mass, axis=1, keepdims=True))
            return 0

        def again(s, _):
            arg = scores_of(wide_ref, blocks_ref, k, s) + beside(bias_ref, s)
            old = scores_ref[0]
            new = jnp.maximum(old, arg)
            scores_ref[1] = scores_ref[1] * jnp.exp(old - new) + jnp.exp(arg - new)
            scores_ref[0] = new
            return 0

        if keep:
            lax.fori_loop(0, columns // strip, over, 0)
        else:
            scores_ref[0] = jnp.full((columns, 2 * rows), LOWEST, jnp.float32)
            scores_ref[1] = jnp.zeros((columns, 2 * rows), jnp.float32)
            lax.fori_loop(0, doubles, again, 0)
            peak = jnp.max(scores_ref[0], axis=1, keepdims=True)
            mass = jnp.sum(scores_ref[1] * jnp.exp(scores_ref[0] - peak), axis=1, keepdims=True)
            column_ref[...] = peak + jnp.log(mass)
        line_ref[k] = column_ref[...].reshape(1, -1)

    for d in range(1, depth):
        there = lax.rem(z + d, depth)
        column(there)
        copy = pltpu.make_async_remote_copy(
            src_ref=line_ref.at[there],
            dst_ref=total_ref.at[z],
            send_sem=line_send.at[d],
            recv_sem=line_recv.at[d],
            device_id=place(there, r, o),
            device_id_type=MESH,
        )
        copy.start()
        outgoing.append(copy)
    column(z)
    total_ref[z] = line_ref[z]
    for d in range(1, depth):
        source = lax.rem(z + depth - d, depth)
        slot = total_ref.at[source]
        pltpu.make_async_remote_copy(
            src_ref=slot,
            dst_ref=slot,
            send_sem=line_send.at[d],
            recv_sem=line_recv.at[d],
            device_id=place(source, r, o),
            device_id_type=MESH,
        ).wait_recv()
    proto_out[...] = -lse(total_ref[...], 0)
    for copy in outgoing:
        copy.wait_send()
    for t in range(depth - 1):
        for n in range(PIECES):
            for up in (True, False):

                @pl.when(sends(t, up))
                def _():
                    for copy in chain(t, up, n):
                        copy.wait_send()


def body(points, prototypes, coarse_duals, active):
    depth = lax.axis_size("z")
    owners = lax.axis_size("proto")
    plane = lax.axis_size("r")
    blocks, rows, width = points.shape
    columns, features = prototypes.shape[1:]
    held = blocks * plane
    hops = plane * owners
    keep = depth * held * rows * columns * 4 <= KEPT_MOST
    vmem = pl.BlockSpec(memory_space=pltpu.VMEM)
    anywhere = pl.BlockSpec(memory_space=pl.ANY)
    dma = pltpu.SemaphoreType.DMA
    real = jnp.float32
    scores = (depth, held // 2, columns, 2 * rows) if keep else (2, columns, 2 * rows)
    return pl.pallas_call(
        functools.partial(fused_kernel, (depth, plane, owners), keep),
        out_shape=(
            jax.ShapeDtypeStruct((blocks, rows), real),
            jax.ShapeDtypeStruct((1, columns), real),
        ),
        in_specs=[anywhere] * 4,
        out_specs=(vmem, vmem),
        scratch_shapes=[
            pltpu.VMEM((plane, owners, blocks, rows, width), points.dtype),
            pltpu.VMEM((depth, columns, features), prototypes.dtype),
            pltpu.VMEM((depth, 1, columns), real),
            pltpu.VMEM((plane,) + active.shape, active.dtype),
            pltpu.VMEM(scores, real),
            pltpu.VMEM((depth, held, rows), real),
            pltpu.VMEM((hops, held, rows), real),
            pltpu.VMEM((held, rows), real),
            pltpu.VMEM((columns, 1), real),
            pltpu.VMEM((depth, 1, columns), real),
            pltpu.VMEM((depth, 1, columns), real),
            pltpu.VMEM((held, rows), real),
            dma((4,)),
        ]
        + [dma((depth, 2 * PIECES))] * 4
        + [dma((hops, 2))] * 4
        + [dma((hops,))] * 2
        + [dma((depth,))] * 2,
        compiler_params=pltpu.CompilerParams(
            collective_id=0, has_side_effects=True, vmem_limit_bytes=VMEM_MOST
        ),
    )(points, prototypes, coarse_duals[None], active)


def solution(mesh):
    groups, owners = mesh.shape["pts"], mesh.shape["proto"]
    plane = PLANE if groups % PLANE == 0 else 1
    grid = Mesh(mesh.devices.reshape(groups // plane, plane, owners), ("z", "r", "proto"))
    pts = ("z", "r")
    both = ("z", "r", "proto")
    return jax.shard_map(
        body,
        mesh=grid,
        in_specs=(P(pts, None, "proto"), P(both, None, None), P(both, None), P(pts, None)),
        out_specs=(P(pts, None), P(both, None)),
        check_vma=False,
    )
```

time: 135 us -> 115 us (0.85)
  Pallas kernels: 128 us -> 112 us
  other arithmetic: 1.62 us -> 0 us
  local copies, waits for them, and re-layouts: 3.32 us -> 1.85 us
    pallas_call x5 -> x1, Pallas kernels: 128 us -> 112 us  [body(): pl.pallas_call(functools.partial(fused_kernel, (depth, plane, owners), ke...]
    reduce_sum x3 -> x0, other arithmetic: 1.51 us -> none  [the longest x1 0.73 us: body(): order = jnp.sum(jnp.where(hit, ids[None, None, :], 0), axis=2)]
where the time goes in v3:
time: 115 us
  Pallas kernels  112 us (97%)
  local copies, waits for them, and re-layouts  1.85 us (2%)
    pallas_call x1, Pallas kernels, body(): pl.pallas_call(functools.partial(fused_kernel, (depth, plane, owners), ke...  112 us

profile of v3, /device:TPU:0, one launch (start us, length us, event | category | flops | bytes accessed | tf_op | source)
XLA Modules:
  0.0 114.8 jit_solution(14531779668203802187)
XLA Ops:
  0.6 112.3 %shard_map.59 = (f32[8,128]{1,0:T(8,128)}, f32[1,512]{1,0:T(1,128)}) custom-call(bf16[8,128,512]{2,1,0:T(8,128)(2,1)} %points_ref.1, bf16[1,512,1024]{2,1,0:T(8,128)(2,1)} %protos_ref.1, f32[1,1,512]{2,1,0:T(1,128)} %bitcast.1, s32[8,8]{1,0:T(8,128)} %active_ref.1), custom_call_target="tpu_custom_call" | custom-call | tf_op jit(solution)/shard_map/pallas_call | solution.py:417
  113.0 0.0 copy-start
  113.0 1.3 %copy.8 = f32[8,128]{1,0:T(8,128)} copy(f32[8,128]{1,0:T(8,128)} %get-tuple-element.4) | data formatting | bytes 8192
  114.2 0.0 copy-done
  114.2 0.6 copy.9
Async XLA Ops:
  113.0 1.3 %copy-start = (f32[1,512]{1,0:T(1,128)S(1)}, f32[1,512]{1,0:T(1,128)}, u32[]{:S(2)}) copy-start(f32[1,512]{1,0:T(1,128)} %get-tuple-element.5) | copy-start | bytes 6148

commit v4 on v3

--- a/solution.py
+++ b/solution.py
@@ -10,6 +10,8 @@
 LOWEST = -1e30
 PLANE = 4
 PIECES = 2
+CUTS = 1
+UNROLL = 4
 KEPT_MOST = 32 * 1024 * 1024
 VMEM_MOST = 60 * 1024 * 1024
 MESH = pl.DeviceIdType.MESH
@@ -20,10 +22,10 @@
     return jnp.concatenate([points_ref[i // blocks, o, i % blocks] for o in range(owners)], axis=1)
 
 
-def scores_of(points_ref, protos_ref, k, s):
+def scores_of(points_ref, protos_ref, k, cut, s):
     rows = jnp.concatenate([block_of(points_ref, 2 * s), block_of(points_ref, 2 * s + 1)], axis=0)
     return lax.dot_general(
-        protos_ref[k], rows, (((1,), (1,)), ((), ())), preferred_element_type=jnp.float32
+        protos_ref[k, cut], rows, (((1,), (1,)), ((), ())), preferred_element_type=jnp.float32
     )
 
 
@@ -93,6 +95,9 @@
 
     moves = [(da, do) for da in range(wings) for do in range(owners) if da or do]
     moves.sort(key=lambda m: (m[0] > 0 and m[1] > 0, m[0] > 0))
+    square = wings == 2 and owners == 2
+    direct = [m for m in moves if not (square and m[0] and m[1])]
+    half = points_ref.shape[0] // 2
     twin = place(z, a * halves + (1 - c), o)
     around = [(dr, do) for dr in range(plane) for do in range(owners) if dr or do]
 
@@ -197,7 +202,7 @@
     for n in range(PIECES):
         start_chain(0, n)
     outgoing = []
-    for n, (da, do) in enumerate(moves):
+    for n, (da, do) in enumerate(direct):
         base, there = shifted(da, do)
         copies = pair(True, r, o, place(z, base + c, there), point_send, point_recv, n, do == 0)
         for copy in copies:
@@ -212,12 +217,33 @@
     for copy in local:
         copy.start()
 
+    def corner(m, da, do, target):
+        base, at_o = shifted(da, do)
+        slot = wide_ref.at[base + c, at_o, pl.ds(m * half, half)]
+        return pltpu.make_async_remote_copy(
+            src_ref=slot,
+            dst_ref=slot,
+            send_sem=point_send.at[len(moves) - 1 + m, 0],
+            recv_sem=point_recv.at[len(moves) - 1 + m, 0],
+            device_id=target,
+            device_id_type=MESH,
+        )
+
     def pass_on(n):
         da, do = moves[n]
         base, from_o = shifted(-da, -do)
-        copies = pair(False, base + c, from_o, twin, point_send, point_recv, n, do == 0)
-        for copy in copies:
-            copy.wait_recv()
+        if moves[n] in direct:
+            copies = pair(False, base + c, from_o, twin, point_send, point_recv, n, do == 0)
+            for copy in copies:
+                copy.wait_recv()
+            if square:
+                ahead, there = shifted(1 - da, 1 - do)
+                copy = corner(do, da, do, place(z, ahead + c, there))
+                copy.start()
+                outgoing.append(copy)
+        else:
+            for m in range(2):
+                corner(m, 1, 1, place(z, r, o)).wait_recv()
         if halves == 2:
             copies = pair(False, base + c, from_o, twin, hop_send, hop_recv, n, do == 0)
             for copy in copies:
@@ -238,46 +264,48 @@
     held, rows = all_ref.shape[1:]
     columns = blocks_ref.shape[1]
     doubles = held // 2
+    cut_rows = columns // CUTS
 
     def named(k):
         block = (k * plane + r) * owners + o
         tags = targets_ref[...].reshape(held, targets_ref.shape[2])
         return jnp.max(jnp.where(tags == block, 1.0, 0.0), axis=1, keepdims=True) > 0.0
 
-    def score(k):
-        coarse = duals_ref[k].reshape(-1, 1)
+    def score(k, n):
+        coarse = duals_ref[k, :, pl.ds(n * cut_rows, cut_rows)].reshape(-1, 1)
+        spots = k * CUTS + n
 
         def step(s, _):
-            found = scores_of(wide_ref, blocks_ref, k, s)
+            found = scores_of(wide_ref, blocks_ref, k, pl.ds(n * cut_rows, cut_rows), s)
             if keep:
-                scores_ref[k, s] = found
+                scores_ref[k, n, s] = found
             given = found + coarse
             peak = jnp.max(given, axis=0, keepdims=True)
             value = peak + jnp.log(jnp.sum(jnp.exp(given - peak), axis=0, keepdims=True))
-            part_ref[k, pl.ds(2 * s, 1)] = value[:, :rows]
-            part_ref[k, pl.ds(2 * s + 1, 1)] = value[:, rows:]
+            part_ref[spots, pl.ds(2 * s, 1)] = value[:, :rows]
+            part_ref[spots, pl.ds(2 * s + 1, 1)] = value[:, rows:]
             return 0
 
-        lax.fori_loop(0, doubles, step, 0)
-        part_ref[k] = jnp.where(named(k), part_ref[k], LOWEST)
-
-    def score_step(t):
+        lax.fori_loop(0, doubles, step, 0, unroll=UNROLL)
+        part_ref[spots] = jnp.where(named(k), part_ref[spots], LOWEST)
+
+    def score_step(t, n):
         if t < 0:
-            score(z)
+            score(z, n)
             return
 
-        def side(n, _):
-            slot = z + (1 + t) * (2 * n - 1)
+        def side(m, _):
+            slot = z + (1 + t) * (2 * m - 1)
 
             @pl.when((slot >= 0) & (slot < depth))
             def _():
-                score(slot)
+                score(slot, n)
 
             return 0
 
         lax.fori_loop(0, 2, side, 0)
 
-    todo = list(range(-1, depth - 1))
+    todo = [(t, n) for t in range(-1, depth - 1) for n in range(CUTS)]
     settled = False
     for t in range(depth - 1):
         for n in range(PIECES):
@@ -288,13 +316,13 @@
                 if not settled:
                     settle_points()
                     settled = True
-                limit = t - 1 if n < PIECES - 1 else t
-                if todo and todo[0] <= limit:
-                    score_step(todo.pop(0))
+                if todo and todo[0] <= (t if n == PIECES - 1 else t - 1, CUTS):
+                    for _ in range(CUTS):
+                        score_step(*todo.pop(0))
     if not settled:
         settle_points()
-    for t in todo:
-        score_step(t)
+    for item in todo:
+        score_step(*item)
 
     me = r * owners + o
     all_ref[me] = lse(part_ref[...], 0)
@@ -330,20 +358,20 @@
     def column(k):
         bias_ref[...] = jnp.where(named(k), work_ref[...], LOWEST)
 
-        def over(n, _):
+        def over(part, n, _):
             cut = pl.ds(pl.multiple_of(n * strip, strip), strip)
             peak = jnp.full((strip, 2 * rows), LOWEST, jnp.float32)
             for s in range(doubles):
-                peak = jnp.maximum(peak, scores_ref[k, s, cut] + beside(bias_ref, s))
+                peak = jnp.maximum(peak, scores_ref[k, part, s, cut] + beside(bias_ref, s))
             peak = jnp.max(peak, axis=1, keepdims=True)
             mass = jnp.zeros((strip, 2 * rows), jnp.float32)
             for s in range(doubles):
-                mass = mass + jnp.exp(scores_ref[k, s, cut] + beside(bias_ref, s) - peak)
-            column_ref[cut] = peak + jnp.log(jnp.sum(mass, axis=1, keepdims=True))
+                mass = mass + jnp.exp(scores_ref[k, part, s, cut] + beside(bias_ref, s) - peak)
+            column_ref[pl.ds(pl.multiple_of(part * cut_rows + n * strip, strip), strip)] = peak + jnp.log(jnp.sum(mass, axis=1, keepdims=True))
             return 0
 
         def again(s, _):
-            arg = scores_of(wide_ref, blocks_ref, k, s) + beside(bias_ref, s)
+            arg = scores_of(wide_ref, blocks_ref, k, pl.ds(0, columns), s) + beside(bias_ref, s)
             old = scores_ref[0]
             new = jnp.maximum(old, arg)
             scores_ref[1] = scores_ref[1] * jnp.exp(old - new) + jnp.exp(arg - new)
@@ -351,7 +379,8 @@
             return 0
 
         if keep:
-            lax.fori_loop(0, columns // strip, over, 0)
+            for part in range(CUTS):
+                lax.fori_loop(0, cut_rows // strip, functools.partial(over, part), 0)
         else:
             scores_ref[0] = jnp.full((columns, 2 * rows), LOWEST, jnp.float32)
             scores_ref[1] = jnp.zeros((columns, 2 * rows), jnp.float32)
@@ -413,7 +442,7 @@
     anywhere = pl.BlockSpec(memory_space=pl.ANY)
     dma = pltpu.SemaphoreType.DMA
     real = jnp.float32
-    scores = (depth, held // 2, columns, 2 * rows) if keep else (2, columns, 2 * rows)
+    scores = (depth, CUTS, held // 2, columns // CUTS, 2 * rows) if keep else (2, columns, 2 * rows)
     return pl.pallas_call(
         functools.partial(fused_kernel, (depth, plane, owners), keep),
         out_shape=(
@@ -428,7 +457,7 @@
             pltpu.VMEM((depth, 1, columns), real),
             pltpu.VMEM((plane,) + active.shape, active.dtype),
             pltpu.VMEM(scores, real),
-            pltpu.VMEM((depth, held, rows), real),
+            pltpu.VMEM((depth * CUTS, held, rows), real),
             pltpu.VMEM((hops, held, rows), real),
             pltpu.VMEM((held, rows), real),
             pltpu.VMEM((columns, 1), real),

time: 115 us -> 104 us (0.904)
  Pallas kernels: 112 us -> 101 us
    pallas_call x1, Pallas kernels: 112 us -> 101 us  [body(): pl.pallas_call(functools.partial(fused_kernel, (depth, plane, owners), ke...]
where the time goes in v4:
time: 104 us
  Pallas kernels  101 us (97%)
  local copies, waits for them, and re-layouts  1.85 us (2%)
    pallas_call x1, Pallas kernels, body(): pl.pallas_call(functools.partial(fused_kernel, (depth, plane, owners), ke...  101 us

profile of v4, /device:TPU:0, one launch (start us, length us, event | category | flops | bytes accessed | tf_op | source)
XLA Modules:
  0.0 103.8 jit_solution(3334252695597158629)
XLA Ops:
  0.6 101.4 %shard_map.59 = (f32[8,128]{1,0:T(8,128)}, f32[1,512]{1,0:T(1,128)}) custom-call(bf16[8,128,512]{2,1,0:T(8,128)(2,1)} %points_ref.1, bf16[1,512,1024]{2,1,0:T(8,128)(2,1)} %protos_ref.1, f32[1,1,512]{2,1,0:T(1,128)} %bitcast.1, s32[8,8]{1,0:T(8,128)} %active_ref.1), custom_call_target="tpu_custom_call" | custom-call | tf_op jit(solution)/shard_map/pallas_call | solution.py:446
  102.0 0.0 copy-start
  102.0 1.3 %copy.8 = f32[8,128]{1,0:T(8,128)} copy(f32[8,128]{1,0:T(8,128)} %get-tuple-element.4) | data formatting | bytes 8192
  103.3 0.0 copy-done
  103.3 0.6 copy.9
Async XLA Ops:
  102.0 1.3 %copy-start = (f32[1,512]{1,0:T(1,128)S(1)}, f32[1,512]{1,0:T(1,128)}, u32[]{:S(2)}) copy-start(f32[1,512]{1,0:T(1,128)} %get-tuple-element.5) | copy-start | bytes 6148
